TPU v7x, 512 devices: a whole 4x8x8 slice. The times are simulated.
512 devices in a mesh: dp: 64 (over z_lo, y, x), tensor: 8 (over z_hi, core).
Axes of the slice: x: 4, y: 8, z: 8 (z_hi: 4, z_lo: 2; z = z_hi * 2 + z_lo), core: 2. Of those that a mesh axis runs over, the one named last changes fastest.
Arguments:
- tokens: bfloat16 [8192, 6144], P('dp', 'tensor'), may hold values from -6 to 6
- cotangent: bfloat16 [8192, 6144], P('dp', 'tensor'), may hold values from -6 to 6
- w_gate: bfloat16 [1, 6144, 16384], P(None, 'tensor', 'dp'), may hold values from -0.078125 to 0.078125
- w_up: bfloat16 [1, 6144, 16384], P(None, 'tensor', 'dp'), may hold values from -0.078125 to 0.078125
- w_down: bfloat16 [1, 16384, 6144], P(None, 'dp', 'tensor'), may hold values from -0.046875 to 0.046875
- slot_token: int32 [64, 1, 6], P('dp'), may hold values from -1 to 127, as said below
- route_weight: float32 [64, 1, 6], P('dp'), may hold values from 0.2 to 1
Outputs:
- mixed: bfloat16 [8192, 6144], P('dp', 'tensor')
- grad_tokens: bfloat16 [8192, 6144], P('dp', 'tensor')
- grad_gate: bfloat16 [1, 6144, 16384], P(None, 'tensor', 'dp')
- grad_up: bfloat16 [1, 6144, 16384], P(None, 'tensor', 'dp')
- grad_down: bfloat16 [1, 16384, 6144], P(None, 'dp', 'tensor')
Inputs may be any that keep to these rules, and one draw needn't show every extreme that they name: `slot_token`: for each block and expert the filled slots come first and name distinct tokens of that block; every block has at least one filled slot for each expert, and for each expert some block fills all 6 slots.
All inputs are finite; a program needn't handle non-finite values.
Results may differ from a plain program's by a relative error of at most 0.0057.
Values may be sent and summed in bfloat16 or wider, within the bound.
No kernel may reach another device: no remote copies, remote signals or barrier semaphores. Data moves between devices by JAX's collectives and lax.ppermute only.
A program may use at most 64 MiB of HBM per device.

v0:
```python
import jax
import jax.numpy as jnp
from jax import lax
from jax.sharding import PartitionSpec as P


def on_device(tokens, cotangent, w_gate, w_up, w_down, slot_token, route_weight):
    tok_dev = tokens.shape[0]
    slot_ids = slot_token[0].T
    slot_weights = route_weight[0].T
    usable = slot_ids >= 0
    clipped = jnp.maximum(slot_ids, 0)
    picked = jnp.where(usable[:, :, None], tokens[clipped], 0)
    d_local = (
        slot_weights[:, :, None]
        * cotangent[clipped].astype(jnp.float32)
        * usable[:, :, None].astype(jnp.float32)
    ).astype(jnp.bfloat16)
    all_rows = lax.all_gather(picked, "dp", axis=0, tiled=True)
    gate_part = jnp.einsum("sed,edf->sef", all_rows, w_gate, preferred_element_type=jnp.float32)
    up_part = jnp.einsum("sed,edf->sef", all_rows, w_up, preferred_element_type=jnp.float32)
    gate_sum, up_sum = lax.psum((gate_part, up_part), "tensor")
    sigmoid_gate = jax.nn.sigmoid(gate_sum)
    activated = gate_sum * sigmoid_gate
    hidden = (activated * up_sum).astype(jnp.bfloat16)
    local_combine = (jnp.arange(tok_dev, dtype=jnp.int32)[:, None, None] == slot_ids[None]).astype(
        jnp.float32
    )
    own_rows = lax.psum_scatter(
        jnp.einsum("sef,efd->sed", hidden, w_down, preferred_element_type=jnp.float32),
        "dp",
        scatter_dimension=0,
        tiled=True,
    )
    mixed = jnp.einsum(
        "tce,ced->td", local_combine * slot_weights[None], own_rows, precision=lax.Precision.HIGHEST
    )
    all_grads = lax.all_gather(d_local, "dp", axis=0, tiled=True)
    hidden_part = jnp.einsum("sed,efd->sef", all_grads, w_down, preferred_element_type=jnp.float32)
    hidden_grad = lax.psum(hidden_part, "tensor")
    d_gate = (hidden_grad * up_sum * sigmoid_gate * (1.0 + gate_sum * (1.0 - sigmoid_gate))).astype(
        jnp.bfloat16
    )
    d_up = (hidden_grad * activated).astype(jnp.bfloat16)
    grad_down = jnp.einsum(
        "sef,sed->efd", hidden, all_grads, preferred_element_type=jnp.float32
    ).astype(jnp.bfloat16)
    grad_gate = jnp.einsum(
        "sed,sef->edf", all_rows, d_gate, preferred_element_type=jnp.float32
    ).astype(jnp.bfloat16)
    grad_up = jnp.einsum("sed,sef->edf", all_rows, d_up, preferred_element_type=jnp.float32).astype(
        jnp.bfloat16
    )
    own_grads = lax.psum_scatter(
        jnp.einsum("sef,edf->sed", d_gate, w_gate, preferred_element_type=jnp.float32)
        + jnp.einsum("sef,edf->sed", d_up, w_up, preferred_element_type=jnp.float32),
        "dp",
        scatter_dimension=0,
        tiled=True,
    )
    grad_tokens = jnp.einsum(
        "tce,ced->td", local_combine, own_grads, precision=lax.Precision.HIGHEST
    )
    return (
        mixed.astype(jnp.bfloat16),
        grad_tokens.astype(jnp.bfloat16),
        grad_gate,
        grad_up,
        grad_down,
    )


def solution(mesh):
    return jax.shard_map(
        on_device,
        mesh=mesh,
        in_specs=(
            P("dp", "tensor"),
            P("dp", "tensor"),
            P(None, "tensor", "dp"),
            P(None, "tensor", "dp"),
            P(None, "dp", "tensor"),
            P("dp", None, None),
            P("dp", None, None),
        ),
        out_specs=(
            P("dp", "tensor"),
            P("dp", "tensor"),
            P(None, "tensor", "dp"),
            P(None, "tensor", "dp"),
            P(None, "dp", "tensor"),
        ),
        check_vma=False,
    )
```

profile of v0, /device:TPU:64, one launch (start us, length us, event | category | flops | bytes accessed | tf_op | source)
XLA Modules:
  0.0 1044.3 jit_solution(7480080014284035748)
XLA Ops:
  7.2 0.7 maximum_bitcast_fusion
  7.9 0.7 fusion.37
  8.6 1.5 gather_fusion.1
  10.1 0.7 fusion.30
  10.9 1.5 gather_fusion
  12.5 161.2 %all_gather.7 = bf16[384,1,768]{2,1,0:T(2,128)(2,1)S(1)} all-gather(bf16[6,1,768]{2,1,0:T(2,128)(2,1)S(1)} %copy.18), channel_id=1, replica_groups=mesh['dp'=64,'tensor'=8] {'dp'}, dimensions={0}, use_global_device_ids=true | all-gather | bytes 599040 | tf_op jit(solution)/shard_map/all_gather | solution.py:38
  173.7 156.4 %all_gather.6 = bf16[384,1,768]{2,1,0:T(2,128)(2,1)S(1)} all-gather(bf16[6,1,768]{2,1,0:T(2,128)(2,1)S(1)} %copy.16), channel_id=1, replica_groups=mesh['dp'=64,'tensor'=8] {'dp'}, dimensions={0}, use_global_device_ids=true | all-gather | bytes 599040 | tf_op jit(solution)/shard_map/all_gather | solution.py:19
  330.2 0.9 copy-done.2
  331.1 1.1 convolution_bitcast_fusion.2
  332.2 1.1 convolution_bitcast_fusion.3
  333.2 1.1 convolution_bitcast_fusion.1
  334.4 81.8 %all-reduce.9.cloned.1.call-done = (f32[384,1,256]{2,0,1:T(8,128)}, f32[384,1,256]{2,0,1:T(8,128)}, f32[384,1,256]{2,0,1:T(8,128)}) async-done(((f32[384,1,256]{2,0,1:T(8,128)}, f32[384,1,256]{2,0,1:T(8,128)}, f32[384,1,256]{2,0,1:T(8,128)}), (f32[384,1,256]{2,0,1:T(8,128)}, f32[384,1,256]{2,0,1:T(8,128)}, f32[384,1,256]{2,0,1:T(8,128)})) %all-reduce.9.cloned.1.call-update) | async-done | bytes 1179664 | tf_op jit(solution)/shard_map/psum | solution.py:22
  416.2 1.5 fusion.21
  418.0 0.3 fusion
  418.4 2.2 copy.19
  420.9 2.2 copy.17
  423.2 1.3 dynamic-slice
  425.1 1.1 fusion.3
  426.2 1.2 fusion.2
  427.4 1.2 fusion.1
  428.6 605.9 %all-reduce.7.cloned.1.call-done = (f32[384,1,768]{2,1,0:T(1,128)}, f32[384,1,768]{2,1,0:T(1,128)}) async-done(((f32[384,1,768]{2,1,0:T(1,128)}, f32[384,1,768]{2,1,0:T(1,128)}), (f32[384,1,768]{2,1,0:T(1,128)}, f32[384,1,768]{2,1,0:T(1,128)})) %all-reduce.7.cloned.1.call-update) | async-done | bytes 2359312
  1034.4 0.7 constant_dynamic-slice_fusion
  1035.2 1.0 convolution_convert_fusion.3
  1036.2 1.3 convolution_convert_fusion.4
  (20 shorter events, 1.0 us)
Async XLA Ops:
  7.2 325.0 %copy-start = (bf16[1,768,256]{2,1,0:T(8,128)(2,1)S(1)}, bf16[1,768,256]{2,1,0:T(8,128)(2,1)}, u32[]{:S(2)}) copy-start(bf16[1,768,256]{2,1,0:T(8,128)(2,1)} %param.9) | copy-start | bytes 1179652
  7.2 409.0 %all-reduce.9.cloned.1.call-start = ((), (), s32[]{:S(2)}) async-start(), calls=%async_computation.1 | async-start | bytes 2359296 | tf_op jit(solution)/shard_map/psum | solution.py:22
  330.1 1.0 copy-start.2
  331.1 2.1 copy-start.1
  334.4 700.1 %all-reduce.7.cloned.1.call-start = ((), (), s32[]{:S(2)}) async-start(), calls=%async_computation | async-start | bytes 4718592
  426.2 608.9 %copy-start.3 = (s32[1,1,6]{2,1,0:T(1,128)S(1)}, s32[1,1,6]{2,1,0:T(1,128)}, u32[]{:S(2)}) copy-start(s32[1,1,6]{2,1,0:T(1,128)} %param.12) | copy-start | bytes 76
  426.2 609.9 %copy-start.4 = (f32[1,1,6]{2,1,0:T(1,128)S(1)}, f32[1,1,6]{2,1,0:T(1,128)}, u32[]{:S(2)}) copy-start(f32[1,1,6]{2,1,0:T(1,128)} %param.13) | copy-start | bytes 76
Sparse Core Ops, SparseCore 0:
  334.5 81.6 all-reduce.8
  423.3 611.0 all-reduce.6
where the time goes:
time: 1040 us
  waiting for transfers between devices  688 us (66%)
  blocking collectives  318 us (31%)
  between operations  14.8 us (1%)
  local copies, waits for them, and re-layouts  10.6 us (1%)
    unnamed x3, waiting for transfers between devices  606 us
    all_gather x1, blocking collectives, on_device(): all_grads = lax.all_gather(d_local, 'dp', axis=0, tiled=True)  161 us
    all_gather x1, blocking collectives, on_device(): all_rows = lax.all_gather(picked, 'dp', axis=0, tiled=True)  156 us
    psum x1, waiting for transfers between devices, on_device(): gate_sum, up_sum = lax.psum((gate_part, up_part), 'tensor')  81.8 us
  transfers between devices with their start and end apart: 2, of which 2 were waited for; matrix products, arithmetic and copies ran while one was open for 0% of the time, Pallas kernels for 0%

commit v1 on v0

--- a/solution.py
+++ b/solution.py
@@ -16,7 +16,9 @@
         * cotangent[clipped].astype(jnp.float32)
         * usable[:, :, None].astype(jnp.float32)
     ).astype(jnp.bfloat16)
-    all_rows = lax.all_gather(picked, "dp", axis=0, tiled=True)
+    all_rows = jnp.concatenate(
+        lax.all_to_all(jnp.stack([picked] * lax.axis_size("dp")), "dp", 0, 0), axis=0
+    )
     gate_part = jnp.einsum("sed,edf->sef", all_rows, w_gate, preferred_element_type=jnp.float32)
     up_part = jnp.einsum("sed,edf->sef", all_rows, w_up, preferred_element_type=jnp.float32)
     gate_sum, up_sum = lax.psum((gate_part, up_part), "tensor")

time: 1040 us -> 908 us (0.87)
  blocking collectives: 318 us -> 169 us
  starting transfers between devices: 0.08 us -> 11.9 us
    all_gather x1 -> x0, blocking collectives: 156 us -> none  [on_device(): all_rows = lax.all_gather(picked, 'dp', axis=0, tiled=True)]
    all_to_all x0 -> x1, starting transfers between devices: none -> 11.8 us  [on_device(): lax.all_to_all(jnp.stack([picked] * lax.axis_size('dp')), 'dp', 0, 0)]
  transfers between devices with their start and end apart: 2 -> 3, of which waited for: 2 -> 2; matrix products, arithmetic and copies ran while one was open for 0% -> 1% of each run, Pallas kernels for 0% -> 0%
where the time goes in v1:
time: 908 us; the launch traced here: 907 us
  waiting for transfers between devices  687 us (76%)
  blocking collectives  169 us (19%)
  between operations  14.8 us (2%)
  starting transfers between devices  11.9 us (1%)
  matrix products  10.9 us (1%)
  local copies, waits for them, and re-layouts  10.4 us (1%)
    unnamed x3, waiting for transfers between devices  606 us
    all_gather x1, blocking collectives, on_device(): all_grads = lax.all_gather(d_local, 'dp', axis=0, tiled=True)  169 us
    psum x1, waiting for transfers between devices, on_device(): gate_sum, up_sum = lax.psum((gate_part, up_part), 'tensor')  81.1 us
  transfers between devices with their start and end apart: 3, of which 2 were waited for; matrix products, arithmetic and copies ran while one was open for 1% of the time, Pallas kernels for 0%

profile of v1, /device:TPU:64, one launch (start us, length us, event | category | flops | bytes accessed | tf_op | source)
XLA Modules:
  0.0 907.4 jit_solution(9491850191794851445)
XLA Ops:
  7.2 0.7 maximum_bitcast_fusion
  7.9 0.7 fusion.33
  8.6 1.5 gather_fusion
  10.2 1.0 stack.2
  11.1 11.8 %all-to-all-start = ((bf16[64,6,1,768]{3,1,2,0:T(8,128)(2,1)}), bf16[64,6,1,768]{3,1,2,0:T(8,128)(2,1)S(1)}, u32[]{:S(2)}, u32[]{:S(2)}) async-start(bf16[64,6,1,768]{3,1,2,0:T(8,128)(2,1)} %stack.2), calls=%async_computation | async-start | bytes 1572864 | tf_op jit(solution)/shard_map/all_to_all | solution.py:20
  23.0 0.6 gather_fusion.1
  23.7 169.3 %all_gather.3 = bf16[384,1,768]{2,1,0:T(2,128)(2,1)S(1)} all-gather(bf16[6,1,768]{2,1,0:T(2,128)(2,1)S(1)} %copy.16), channel_id=1, replica_groups=mesh['dp'=64,'tensor'=8] {'dp'}, dimensions={0}, use_global_device_ids=true | all-gather | bytes 599040 | tf_op jit(solution)/shard_map/all_gather | solution.py:40
  193.0 1.1 convolution_bitcast_fusion.1
  194.3 2.1 convolution_bitcast_fusion.2
  196.4 1.1 convolution_bitcast_fusion.3
  197.5 81.1 %all-reduce.9.cloned.1.call-done = (f32[384,1,256]{2,0,1:T(8,128)}, f32[384,1,256]{2,0,1:T(8,128)}, f32[384,1,256]{2,0,1:T(8,128)}) async-done(((f32[384,1,256]{2,0,1:T(8,128)}, f32[384,1,256]{2,0,1:T(8,128)}, f32[384,1,256]{2,0,1:T(8,128)}), (f32[384,1,256]{2,0,1:T(8,128)}, f32[384,1,256]{2,0,1:T(8,128)}, f32[384,1,256]{2,0,1:T(8,128)})) %all-reduce.9.cloned.1.call-update) | async-done | bytes 1179664 | tf_op jit(solution)/shard_map/psum | solution.py:24
  278.7 1.5 fusion.17
  280.2 0.3 fusion.10
  280.5 0.6 copy-done.2
  281.5 2.2 copy.17
  284.1 2.2 copy.15
  286.3 1.3 dynamic-slice
  288.3 1.1 fusion.3
  289.4 1.2 fusion.2
  290.5 1.2 fusion.1
  291.7 605.9 %all-reduce.7.cloned.1.call-done = (f32[384,1,768]{2,1,0:T(1,128)}, f32[384,1,768]{2,1,0:T(1,128)}) async-done(((f32[384,1,768]{2,1,0:T(1,128)}, f32[384,1,768]{2,1,0:T(1,128)}), (f32[384,1,768]{2,1,0:T(1,128)}, f32[384,1,768]{2,1,0:T(1,128)})) %all-reduce.7.cloned.1.call-update) | async-done | bytes 2359312
  897.6 0.7 constant_dynamic-slice_fusion
  898.3 1.0 convolution_convert_fusion.3
  899.3 1.3 convolution_convert_fusion.4
  (23 shorter events, 1.2 us)
Async XLA Ops:
  7.2 189.2 %copy-start = (bf16[1,768,256]{2,1,0:T(8,128)(2,1)S(1)}, bf16[1,768,256]{2,1,0:T(8,128)(2,1)}, u32[]{:S(2)}) copy-start(bf16[1,768,256]{2,1,0:T(8,128)(2,1)} %param.9) | copy-start | bytes 1179652
  10.2 12.8 %copy-start.3 = (bf16[128,768]{1,0:T(8,128)(2,1)S(1)}, bf16[128,768]{1,0:T(8,128)(2,1)}, u32[]{:S(2)}) copy-start(bf16[128,768]{1,0:T(8,128)(2,1)} %param.8) | copy-start | bytes 589828
  10.2 13.4 %copy-start.5 = (f32[1,1,6]{2,1,0:T(1,128)S(1)}, f32[1,1,6]{2,1,0:T(1,128)}, u32[]{:S(2)}) copy-start(f32[1,1,6]{2,1,0:T(1,128)} %param.13) | copy-start | bytes 76
  11.1 181.9 %copy-start.1 = (bf16[1,256,768]{2,1,0:T(8,128)(2,1)S(1)}, bf16[1,256,768]{2,1,0:T(8,128)(2,1)}, u32[]{:S(2)}) copy-start(bf16[1,256,768]{2,1,0:T(8,128)(2,1)} %param.11) | copy-start | bytes 1179652
  11.1 183.0 %all-to-all-start = ((bf16[64,6,1,768]{3,1,2,0:T(8,128)(2,1)}), bf16[64,6,1,768]{3,1,2,0:T(8,128)(2,1)S(1)}, u32[]{:S(2)}, u32[]{:S(2)}) async-start(bf16[64,6,1,768]{3,1,2,0:T(8,128)(2,1)} %stack.2), calls=%async_computation | async-start | bytes 1572864 | tf_op jit(solution)/shard_map/all_to_all | solution.py:20
  22.9 255.7 %all-reduce.9.cloned.1.call-start = ((), (), s32[]{:S(2)}) async-start(), calls=%async_computation.2 | async-start | bytes 2359296 | tf_op jit(solution)/shard_map/psum | solution.py:24
  197.5 700.1 %all-reduce.7.cloned.1.call-start = ((), (), s32[]{:S(2)}) async-start(), calls=%async_computation.1 | async-start | bytes 4718592
  280.1 1.0 copy-start.2
  289.4 608.9 %copy-start.4 = (s32[1,1,6]{2,1,0:T(1,128)S(1)}, s32[1,1,6]{2,1,0:T(1,128)}, u32[]{:S(2)}) copy-start(s32[1,1,6]{2,1,0:T(1,128)} %param.12) | copy-start | bytes 76
Sparse Core Ops, SparseCore 0:
  197.6 81.0 all-reduce.8
  286.4 611.0 all-reduce.6
